TPU v7x, 128 devices: a whole 4x4x4 slice. The times are simulated.
128 devices in a mesh: lat: 8 (over y_hi, z), lon: 16 (over x, y_lo, core).
Axes of the slice: x: 4, y: 4 (y_hi: 2, y_lo: 2; y = y_hi * 2 + y_lo), z: 4, core: 2. Of those that a mesh axis runs over, the one named last changes fastest.
Arguments:
- fields: bfloat16 [2, 256, 768, 256], P(None, 'lat', 'lon'), may hold values from -6 to 6
- kernel: bfloat16 [9, 256, 256], replicated, may hold values from -0.125 to 0.125
- conv_bias: float32 [256], replicated, may hold values from -3 to 3
- cotangent: bfloat16 [2, 128, 384, 256], P(None, 'lat', 'lon'), may hold values from -6 to 6
Outputs:
- pooled: bfloat16 [2, 128, 384, 256], P(None, 'lat', 'lon')
- grad_input: bfloat16 [2, 256, 768, 256], P(None, 'lat', 'lon')
- grad_kernel: float32 [9, 256, 256], replicated
- grad_bias: float32 [256], replicated
All inputs are finite; a program needn't handle non-finite values.
Results may differ from a plain program's by a relative error of at most 0.013.
Values may be sent and summed in bfloat16 or wider, within the bound.
No kernel may reach another device: no remote copies, remote signals or barrier semaphores. Data moves between devices by JAX's collectives and lax.ppermute only.
A program may use at most 64 MiB of HBM per device.

v0:
```python
import math
import jax
import jax.numpy as jnp
from jax import lax
from jax.sharding import PartitionSpec as P


def shifted(shard, axis, by):
    size = lax.axis_size(axis)
    return lax.ppermute(shard, axis, [(i, (i + by) % size) for i in range(size)])


def with_halo(shard, sides, width, wrap):
    for axis, dim in sides:
        size, length = (lax.axis_size(axis), shard.shape[dim])
        up = [(i, (i + 1) % size) for i in range(size if wrap else size - 1)]
        down = [(j, i) for i, j in up]
        last = lax.slice_in_dim(shard, length - width, length, axis=dim)
        first = lax.slice_in_dim(shard, 0, width, axis=dim)
        before = lax.ppermute(last, axis, up)
        after = lax.ppermute(first, axis, down)
        shard = jnp.concatenate([before, shard, after], axis=dim)
    return shard


def lat_cosine(rows, first, total):
    index_rows = (first + jnp.arange(rows)).astype(jnp.float32)
    return jnp.cos((index_rows + 0.5) * (math.pi / total) - math.pi / 2)


def extend(field):
    lat_count = lax.axis_size("lat")
    lat_place = lax.axis_index("lat")
    lon_count = lax.axis_size("lon")
    north_row = field[:, :1]
    south_row = field[:, -1:]
    mirror_north, mirror_south = shifted((north_row, south_row), "lon", lon_count // 2)
    rim_rows = with_halo(field, (("lat", 1),), 1, False)
    upper_pad = jnp.where(lat_place == 0, mirror_north, rim_rows[:, :1])
    bottom = jnp.where(lat_place == lat_count - 1, mirror_south, rim_rows[:, -1:])
    tall = jnp.concatenate([upper_pad, field, bottom], axis=1)
    return with_halo(tall, (("lon", 2),), 1, True)


def forward_conv(padded, kernel, rows, cols):
    chans = padded.shape[-1]
    total = jnp.zeros((padded.shape[0] * rows * cols, kernel.shape[2]), jnp.float32)
    for row_off in range(3):
        for col_off in range(3):
            window = padded[:, row_off : row_off + rows, col_off : col_off + cols, :].reshape(
                -1, chans
            )
            total = total + jnp.dot(
                window, kernel[3 * row_off + col_off], preferred_element_type=jnp.float32
            )
    return total.reshape(padded.shape[0], rows, cols, kernel.shape[2])


def back_conv(padded, kernel, rows, cols):
    chans = padded.shape[-1]
    total = jnp.zeros((padded.shape[0] * rows * cols, kernel.shape[1]), jnp.float32)
    for row_off in range(3):
        for col_off in range(3):
            window = padded[
                :, 2 - row_off : 2 - row_off + rows, 2 - col_off : 2 - col_off + cols, :
            ].reshape(-1, chans)
            total = total + lax.dot_general(
                window,
                kernel[3 * row_off + col_off],
                (((1,), (1,)), ((), ())),
                preferred_element_type=jnp.float32,
            )
    return total.reshape(padded.shape[0], rows, cols, kernel.shape[1])


def pole_term(pad_row, kernel, row_off, cols):
    chans = pad_row.shape[-1]
    total = jnp.zeros((pad_row.shape[0] * cols, kernel.shape[1]), jnp.float32)
    for col_off in range(3):
        window = pad_row[:, :, 2 - col_off : 2 - col_off + cols, :].reshape(-1, chans)
        total = total + lax.dot_general(
            window,
            kernel[3 * row_off + col_off],
            (((1,), (1,)), ((), ())),
            preferred_element_type=jnp.float32,
        )
    return total.reshape(pad_row.shape[0], 1, cols, kernel.shape[1])


def kernel_grad(padded, grad_pre, rows, cols):
    chans = padded.shape[-1]
    flat_grad = grad_pre.reshape(-1, grad_pre.shape[-1])
    pieces = []
    for row_off in range(3):
        for col_off in range(3):
            window = padded[:, row_off : row_off + rows, col_off : col_off + cols, :].reshape(
                -1, chans
            )
            pieces.append(
                lax.dot_general(
                    window, flat_grad, (((0,), (0,)), ((), ())), preferred_element_type=jnp.float32
                )
            )
    return jnp.stack(pieces, axis=0)


def local(fields, kernel, conv_bias, cotangent):
    batches, rows, cols, chans = fields.shape
    lat_count = lax.axis_size("lat")
    lat_place = lax.axis_index("lat")
    padded = extend(fields)
    pre = forward_conv(padded, kernel, rows, cols) + conv_bias
    sigma = jax.nn.sigmoid(pre)
    active = (pre * sigma).astype(jnp.bfloat16)
    cosine = lat_cosine(rows, lat_place * rows, rows * lat_count)
    pair_sum = cosine[0::2] + cosine[1::2]
    weighted = active.astype(jnp.float32) * cosine[None, :, None, None]
    pooled = (
        weighted.reshape(batches, rows // 2, 2, cols // 2, 2, chans).sum(axis=(2, 4))
        / (2.0 * pair_sum)[None, :, None, None]
    )
    share = cosine / (2.0 * jnp.repeat(pair_sum, 2))
    spread = jnp.repeat(jnp.repeat(cotangent.astype(jnp.float32), 2, axis=1), 2, axis=2)
    grad_pre = (spread * share[None, :, None, None] * sigma * (1.0 + pre * (1.0 - sigma))).astype(
        jnp.bfloat16
    )
    kernel_part = kernel_grad(padded, grad_pre, rows, cols)
    bias_part = jnp.sum(grad_pre.astype(jnp.float32), axis=(0, 1, 2))
    grad_kernel, grad_bias = lax.psum((kernel_part, bias_part), ("lat", "lon"))
    grad_padded = extend(grad_pre)
    is_north = lat_place == 0
    is_south = lat_place == lat_count - 1
    blank = jnp.zeros_like(grad_padded[:, :1])
    upper_rows = jnp.where(is_north, blank, grad_padded[:, :1])
    lower_rows = jnp.where(is_south, blank, grad_padded[:, -1:])
    inner = jnp.concatenate([upper_rows, grad_padded[:, 1:-1], lower_rows], axis=1)
    back = back_conv(inner, kernel, rows, cols)
    north_add = jnp.where(is_north, pole_term(grad_padded[:, :1], kernel, 0, cols), 0.0)
    south_add = jnp.where(is_south, pole_term(grad_padded[:, -1:], kernel, 2, cols), 0.0)
    back = jnp.concatenate(
        [back[:, :1] + north_add, back[:, 1:-1], back[:, -1:] + south_add], axis=1
    )
    return (pooled.astype(jnp.bfloat16), back.astype(jnp.bfloat16), grad_kernel, grad_bias)


def solution(mesh):
    return jax.shard_map(
        local,
        mesh=mesh,
        in_specs=(P(None, "lat", "lon", None), P(), P(), P(None, "lat", "lon", None)),
        out_specs=(P(None, "lat", "lon", None), P(None, "lat", "lon", None), P(), P()),
        check_vma=False,
    )
```

profile of v0, /device:TPU:1, one launch (start us, length us, event | category | flops | bytes accessed | tf_op | source)
XLA Modules:
  0.0 244.1 jit_solution(9984950914171488139)
XLA Ops:
  8.0 3.6 %collective-permute-start.2 = (bf16[2,1,48,256]{3,2,1,0:T(8,128)(2,1)S(1)}, bf16[2,1,48,256]{3,2,1,0:T(8,128)(2,1)S(1)}, u32[]{:S(2)}, u32[]{:S(2)}) collective-permute-start(bf16[2,1,48,256]{3,2,1,0:T(8,128)(2,1)S(1)} %get-tuple-element.41), channel_id=1, source_target_pairs={{0,8},{1,9},{2,10},{3,11},{4,12},{5,13},{6,14},{7,15},{8,0},{9,1},... | collective-permute-start | bytes 147464 | tf_op jit(solution)/shard_map/ppermute | solution.py:10
  11.7 3.5 %collective-permute-start.1 = (bf16[2,1,48,256]{3,2,1,0:T(8,128)(2,1)S(1)}, bf16[2,1,48,256]{3,2,1,0:T(8,128)(2,1)S(1)}, u32[]{:S(2)}, u32[]{:S(2)}) collective-permute-start(bf16[2,1,48,256]{3,2,1,0:T(8,128)(2,1)S(1)} %get-tuple-element.41), channel_id=1, source_target_pairs={{0,16},{16,32},{32,48},{48,64},{64,80},{80,96},{96,112},{1,17},{17... | collective-permute-start | bytes 147464 | tf_op jit(solution)/shard_map/ppermute | solution.py:20
  18.5 1.7 broadcast_in_dim.22
  20.3 3.4 %reshape.184 = f32[3072,256]{1,0:T(8,128)} reshape(f32[2,32,24,2,256]{4,3,2,1,0:T(2,128)S(1)} %broadcast_in_dim.22) | data formatting | bytes 6291456 | tf_op jit(solution)/shard_map/reshape | solution.py:123
  23.7 3.4 %reshape.178 = f32[2,32,48,256]{3,2,1,0:T(8,128)} reshape(f32[2,32,24,2,256]{4,3,2,1,0:T(2,128)S(1)} %broadcast_in_dim.22) | data formatting | bytes 6291456 | tf_op jit(solution)/shard_map/reshape | solution.py:123
  28.8 1.6 collective-permute-start.5
  30.4 1.4 collective-permute-start.4
  34.9 3.1 %fusion.104 = (bf16[2,32,48,256]{3,2,1,0:T(8,128)(2,1)S(1)}, bf16[2,32,48,256]{3,2,1,0:T(8,128)(2,1)S(1)}, bf16[2,32,48,256]{3,2,1,0:T(8,128)(2,1)S(1)}, bf16[2,...) fusion(bf16[2,34,49,256]{3,2,1,0:T(8,128)(2,1)S(1)} %get-tuple-element., ...), kind=kLoop, calls=%fused_computation.171 | loop fusion | bytes 18874368 | tf_op jit(solution)/shard_map/slice | solution.py:50
  43.4 2.2 convert_reduce_fusion
  45.6 1.4 multiply_convert_fusion.2
  49.2 2.8 %collective-permute-start.6 = (bf16[2,1,48,256]{3,2,1,0:T(8,128)(2,1)}, bf16[2,1,48,256]{3,2,1,0:T(8,128)(2,1)}, u32[]{:S(2)}, u32[]{:S(2)}) collective-permute-start(bf16[2,1,48,256]{3,2,1,0:T(8,128)(2,1)} %get-tuple-element.37), channel_id=1, source_target_pairs={{0,8},{1,9},{2,10},{3,11},{4,12},{5,13},{6,14},{7,15},{8,0},{9,1},... | collective-permute-start | bytes 147464 | tf_op jit(solution)/shard_map/ppermute | solution.py:10
  52.3 5.4 %collective-permute-start.7 = (bf16[2,1,48,256]{3,2,1,0:T(8,128)(2,1)}, bf16[2,1,48,256]{3,2,1,0:T(8,128)(2,1)}, u32[]{:S(2)}, u32[]{:S(2)}) collective-permute-start(bf16[2,1,48,256]{3,2,1,0:T(8,128)(2,1)} %get-tuple-element.38), channel_id=1, source_target_pairs={{0,16},{16,32},{32,48},{48,64},{64,80},{80,96},{96,112},{1,17},{17... | collective-permute-start | bytes 147464 | tf_op jit(solution)/shard_map/ppermute | solution.py:20
  59.0 5.2 %reshape.176 = f32[2,16,2,24,2,256]{5,4,3,2,1,0:T(2,128)} reshape(f32[3072,256]{1,0:T(8,128)} %copy-done.4) | data formatting | bytes 6291456 | tf_op jit(solution)/shard_map/reshape | solution.py:56
  64.2 2.8 %fusion.31 = f32[9,256,256]{2,1,0:T(8,128)} fusion(f32[9,256,256]{2,1,0:T(8,128)} %fusion.21, bf16[2,32,48,256]{3,2,1,0:T(8,128)(2,1)S(1)} %multiply_convert_fusion.2, bf16[2,32,48,256]{3,2,1,0:T(8,128)(2,1)} %param.4, bf16[2,1,48,256]{3,2,1,0:T(8,128)(2,1)} %copy-done.14), kind=kOutput, calls=%fused_computation.76 | convolution fusion | flops 405897216 | bytes 3457024 | tf_op jit(solution)/shard_map/dot_general | solution.py:100
  69.8 1.4 fusion.18
  77.3 3.2 %multiply_reduce_fusion = f32[2,16,24,256]{3,2,1,0:T(8,128)S(1)} fusion(f32[16,2]{1,0:T(8,128)S(1)} %add_cosine_fusion, f32[256]{0:T(256)S(1)} %copy-done.18, f32[2,16,2,24,2,256]{5,4,3,2,1,0:T(2,128)} %reshape.176), kind=kLoop, calls=%fused_computation.23 | loop fusion | flops 6881280 | bytes 3933312 | tf_op jit(solution)/shard_map/reduce_sum | solution.py:119
  81.4 72.1 %psum.15 = f32[256]{0:T(256)} all-reduce(f32[256]{0:T(256)S(1)} %copy-done.21), channel_id=1, replica_groups=mesh['lat'=8,'lon'=16] {'lat','lon'}, use_global_device_ids=true, to_apply=%region_3.4 | all-reduce | flops 256 | bytes 2048 | tf_op jit(solution)/shard_map/psum | solution.py:129
  156.3 1.6 collective-permute-start.10
  158.1 1.5 collective-permute-done.11
  163.7 2.1 pad_maximum_fusion.3
  170.5 1.5 convolution_add_fusion.4
  175.5 1.3 pad_maximum_fusion.7
  176.8 57.3 %all-reduce.2.cloned.1.call-done = f32[9,256,256]{2,1,0:T(8,128)} async-done(((f32[9,256,256]{2,1,0:T(8,128)}), f32[9,256,256]{2,1,0:T(8,128)}) %all-reduce.2.cloned.1.call-update) | async-done | bytes 2359312 | tf_op jit(solution)/shard_map/psum | solution.py:129
  234.1 3.2 %copy.45 = f32[9,256,256]{2,1,0:T(8,128)} copy(f32[9,256,256]{2,1,0:T(8,128)} %all-reduce.2.cloned.1.call-done) | data formatting | bytes 4718592
  (125 shorter events, 42.7 us)
Async XLA Ops:
  7.2 226.9 %all-reduce.2.cloned.1.call-start = ((), (), s32[]{:S(2)}) async-start(), calls=%async_computation | async-start | bytes 4718592 | tf_op jit(solution)/shard_map/psum | solution.py:129
  8.0 19.7 %collective-permute-start.2 = (bf16[2,1,48,256]{3,2,1,0:T(8,128)(2,1)S(1)}, bf16[2,1,48,256]{3,2,1,0:T(8,128)(2,1)S(1)}, u32[]{:S(2)}, u32[]{:S(2)}) collective-permute-start(bf16[2,1,48,256]{3,2,1,0:T(8,128)(2,1)S(1)} %get-tuple-element.41), channel_id=1, source_target_pairs={{0,8},{1,9},{2,10},{3,11},{4,12},{5,13},{6,14},{7,15},{8,0},{9,1},... | collective-permute-start | bytes 147464 | tf_op jit(solution)/shard_map/ppermute | solution.py:10
  11.7 16.1 %collective-permute-start.1 = (bf16[2,1,48,256]{3,2,1,0:T(8,128)(2,1)S(1)}, bf16[2,1,48,256]{3,2,1,0:T(8,128)(2,1)S(1)}, u32[]{:S(2)}, u32[]{:S(2)}) collective-permute-start(bf16[2,1,48,256]{3,2,1,0:T(8,128)(2,1)S(1)} %get-tuple-element.41), channel_id=1, source_target_pairs={{0,16},{16,32},{32,48},{48,64},{64,80},{80,96},{96,112},{1,17},{17... | collective-permute-start | bytes 147464 | tf_op jit(solution)/shard_map/ppermute | solution.py:20
  15.2 12.5 %collective-permute-start.3 = (bf16[2,1,48,256]{3,2,1,0:T(8,128)(2,1)S(1)}, bf16[2,1,48,256]{3,2,1,0:T(8,128)(2,1)S(1)}, u32[]{:S(2)}, u32[]{:S(2)}) collective-permute-start(bf16[2,1,48,256]{3,2,1,0:T(8,128)(2,1)S(1)} %get-tuple-element.42), channel_id=1, source_target_pairs={{16,0},{32,16},{48,32},{64,48},{80,64},{96,80},{112,96},{17,1},{33... | collective-permute-start | bytes 147464 | tf_op jit(solution)/shard_map/ppermute | solution.py:21
  16.5 11.3 %collective-permute-start = (bf16[2,1,48,256]{3,2,1,0:T(8,128)(2,1)S(1)}, bf16[2,1,48,256]{3,2,1,0:T(8,128)(2,1)S(1)}, u32[]{:S(2)}, u32[]{:S(2)}) collective-permute-start(bf16[2,1,48,256]{3,2,1,0:T(8,128)(2,1)S(1)} %get-tuple-element.42), channel_id=1, source_target_pairs={{0,8},{1,9},{2,10},{3,11},{4,12},{5,13},{6,14},{7,15},{8,0},{9,1},... | collective-permute-start | bytes 147464 | tf_op jit(solution)/shard_map/ppermute | solution.py:10
  17.3 9.9 %copy-start.15 = (f32[32]{0:T(128)}, f32[32]{0:T(128)S(1)}, u32[]{:S(2)}) copy-start(f32[32]{0:T(128)S(1)} %fusion.97) | copy-start | bytes 388
  27.8 5.9 %copy-start.12 = (bf16[2,1,48,256]{3,2,1,0:T(8,128)(2,1)}, bf16[2,1,48,256]{3,2,1,0:T(8,128)(2,1)S(1)}, u32[]{:S(2)}) copy-start(bf16[2,1,48,256]{3,2,1,0:T(8,128)(2,1)S(1)} %broadcast_select_fusion.1) | copy-start | bytes 147460
  28.5 5.2 %copy-start.14 = (bf16[2,1,48,256]{3,2,1,0:T(8,128)(2,1)}, bf16[2,1,48,256]{3,2,1,0:T(8,128)(2,1)S(1)}, u32[]{:S(2)}) copy-start(bf16[2,1,48,256]{3,2,1,0:T(8,128)(2,1)S(1)} %broadcast_select_fusion.3) | copy-start | bytes 147460
  28.6 3.3 %copy-start.8 = (bf16[9,256,256]{2,1,0:T(8,128)(2,1)S(1)}, bf16[9,256,256]{2,1,0:T(8,128)(2,1)}, u32[]{:S(2)}) copy-start(bf16[9,256,256]{2,1,0:T(8,128)(2,1)} %param.5) | copy-start | bytes 3538948
  28.8 4.8 %collective-permute-start.5 = (bf16[2,34,1,256]{3,2,1,0:T(2,128)(2,1)S(1)}, bf16[2,34,1,256]{3,2,1,0:T(2,128)(2,1)S(1)}, u32[]{:S(2)}, u32[]{:S(2)}) collective-permute-start(bf16[2,34,1,256]{3,2,1,0:T(2,128)(2,1)S(1)} %get-tuple-element.35), channel_id=1, source_target_pairs={{1,0},{2,1},{3,2},{4,3},{5,4},{6,5},{7,6},{8,7},{9,8},{10,9},{11,1... | collective-permute-start | bytes 104456 | tf_op jit(solution)/shard_map/ppermute | solution.py:21
  30.4 3.3 %collective-permute-start.4 = (bf16[2,34,1,256]{3,2,1,0:T(2,128)(2,1)S(1)}, bf16[2,34,1,256]{3,2,1,0:T(2,128)(2,1)S(1)}, u32[]{:S(2)}, u32[]{:S(2)}) collective-permute-start(bf16[2,34,1,256]{3,2,1,0:T(2,128)(2,1)S(1)} %get-tuple-element.36), channel_id=1, source_target_pairs={{0,1},{1,2},{2,3},{3,4},{4,5},{5,6},{6,7},{7,8},{8,9},{9,10},{10,1... | collective-permute-start | bytes 104456 | tf_op jit(solution)/shard_map/ppermute | solution.py:20
  34.9 3.1 %copy-start.2 = (bf16[2,34,49,256]{3,2,1,0:T(8,128)(2,1)}, bf16[2,34,49,256]{3,2,1,0:T(8,128)(2,1)S(1)}, u32[]{:S(2)}) copy-start(bf16[2,34,49,256]{3,2,1,0:T(8,128)(2,1)S(1)} %get-tuple-element.33) | copy-start | bytes 5117956
  43.4 2.2 copy-start.16
  48.0 106.5 %collective-permute-start.9 = (bf16[2,1,48,256]{3,2,1,0:T(8,128)(2,1)}, bf16[2,1,48,256]{3,2,1,0:T(8,128)(2,1)}, u32[]{:S(2)}, u32[]{:S(2)}) collective-permute-start(bf16[2,1,48,256]{3,2,1,0:T(8,128)(2,1)} %get-tuple-element.37), channel_id=1, source_target_pairs={{16,0},{32,16},{48,32},{64,48},{80,64},{96,80},{112,96},{17,1},{33... | collective-permute-start | bytes 147464 | tf_op jit(solution)/shard_map/ppermute | solution.py:21
  49.2 104.2 %collective-permute-start.6 = (bf16[2,1,48,256]{3,2,1,0:T(8,128)(2,1)}, bf16[2,1,48,256]{3,2,1,0:T(8,128)(2,1)}, u32[]{:S(2)}, u32[]{:S(2)}) collective-permute-start(bf16[2,1,48,256]{3,2,1,0:T(8,128)(2,1)} %get-tuple-element.37), channel_id=1, source_target_pairs={{0,8},{1,9},{2,10},{3,11},{4,12},{5,13},{6,14},{7,15},{8,0},{9,1},... | collective-permute-start | bytes 147464 | tf_op jit(solution)/shard_map/ppermute | solution.py:10
  52.1 102.4 %collective-permute-start.8 = (bf16[2,1,48,256]{3,2,1,0:T(8,128)(2,1)}, bf16[2,1,48,256]{3,2,1,0:T(8,128)(2,1)}, u32[]{:S(2)}, u32[]{:S(2)}) collective-permute-start(bf16[2,1,48,256]{3,2,1,0:T(8,128)(2,1)} %get-tuple-element.38), channel_id=1, source_target_pairs={{0,8},{1,9},{2,10},{3,11},{4,12},{5,13},{6,14},{7,15},{8,0},{9,1},... | collective-permute-start | bytes 147464 | tf_op jit(solution)/shard_map/ppermute | solution.py:10
  52.3 101.2 %collective-permute-start.7 = (bf16[2,1,48,256]{3,2,1,0:T(8,128)(2,1)}, bf16[2,1,48,256]{3,2,1,0:T(8,128)(2,1)}, u32[]{:S(2)}, u32[]{:S(2)}) collective-permute-start(bf16[2,1,48,256]{3,2,1,0:T(8,128)(2,1)} %get-tuple-element.38), channel_id=1, source_target_pairs={{0,16},{16,32},{32,48},{48,64},{64,80},{80,96},{96,112},{1,17},{17... | collective-permute-start | bytes 147464 | tf_op jit(solution)/shard_map/ppermute | solution.py:20
  64.2 2.9 %copy-start.3 = (bf16[2,34,49,256]{3,2,1,0:T(8,128)(2,1)S(1)}, bf16[2,34,49,256]{3,2,1,0:T(8,128)(2,1)}, u32[]{:S(2)}) copy-start(bf16[2,34,49,256]{3,2,1,0:T(8,128)(2,1)} %copy-done.2) | copy-start | bytes 5117956
  77.3 3.2 %copy-start.20 = (f32[16]{0:T(128)S(1)}, f32[16]{0:T(128)}, u32[]{:S(2)}) copy-start(f32[16]{0:T(128)} %copy-done.19) | copy-start | bytes 196
  77.3 4.1 %copy-start.21 = (f32[256]{0:T(256)S(1)}, f32[256]{0:T(256)}, u32[]{:S(2)}) copy-start(f32[256]{0:T(256)} %get-tuple-element.43) | copy-start | bytes 3076
  77.3 77.0 %copy-start.9 = (bf16[9,256,256]{2,1,0:T(8,128)(2,1)S(1)}, bf16[9,256,256]{2,1,0:T(8,128)(2,1)}, u32[]{:S(2)}) copy-start(bf16[9,256,256]{2,1,0:T(8,128)(2,1)} %param.5) | copy-start | bytes 3538948
  155.4 4.1 %collective-permute-start.11 = (bf16[2,34,1,256]{3,2,1,0:T(2,128)(2,1)S(1)}, bf16[2,34,1,256]{3,2,1,0:T(2,128)(2,1)S(1)}, u32[]{:S(2)}, u32[]{:S(2)}) collective-permute-start(bf16[2,34,1,256]{3,2,1,0:T(2,128)(2,1)S(1)} %get-tuple-element.31), channel_id=1, source_target_pairs={{1,0},{2,1},{3,2},{4,3},{5,4},{6,5},{7,6},{8,7},{9,8},{10,9},{11,1... | collective-permute-start | bytes 104456 | tf_op jit(solution)/shard_map/ppermute | solution.py:21
  156.3 3.3 %collective-permute-start.10 = (bf16[2,34,1,256]{3,2,1,0:T(2,128)(2,1)S(1)}, bf16[2,34,1,256]{3,2,1,0:T(2,128)(2,1)S(1)}, u32[]{:S(2)}, u32[]{:S(2)}) collective-permute-start(bf16[2,34,1,256]{3,2,1,0:T(2,128)(2,1)S(1)} %get-tuple-element.32), channel_id=1, source_target_pairs={{0,1},{1,2},{2,3},{3,4},{4,5},{5,6},{6,7},{7,8},{8,9},{9,10},{10,1... | collective-permute-start | bytes 104456 | tf_op jit(solution)/shard_map/ppermute | solution.py:20
  167.6 2.8 %copy-start.11 = (f32[3072,256]{1,0:T(8,128)S(1)}, f32[3072,256]{1,0:T(8,128)}, u32[]{:S(2)}) copy-start(f32[3072,256]{1,0:T(8,128)} %reshape.184) | copy-start | bytes 9437188
  (12 other events, 18.7 us)
Sparse Core Ops, SparseCore 0:
  76.7 157.3 all-reduce.1
where the time goes:
time: 245 us; the launch traced here: 244 us
  blocking collectives  72.1 us (29%)
  waiting for transfers between devices  60.1 us (25%)
  local copies, waits for them, and re-layouts  30.9 us (13%)
  matrix products  27.7 us (11%)
  starting transfers between devices  24.1 us (10%)
  other arithmetic  14.8 us (6%)
  between operations  14.5 us (6%)
    psum x1, blocking collectives, local(): grad_kernel, grad_bias = lax.psum((kernel_part, bias_part), ('lat', 'lon'))  72.1 us
    psum x1, waiting for transfers between devices, local(): grad_kernel, grad_bias = lax.psum((kernel_part, bias_part), ('lat', 'lon'))  57.3 us
    dot_general x9, matrix products, kernel_grad(): lax.dot_general(window, flat_grad, (((0,), (0,)), ((), ())), preferred_el...  13.5 us
    ppermute x4, starting transfers between devices, with_halo(): before = lax.ppermute(last, axis, up)  12 us
    unnamed x45, local copies, waits for them, and re-layouts  8.65 us
    ppermute x4, starting transfers between devices, shifted(): lax.ppermute(shard, axis, [(i, (i + by) % size) for i in range(size)])  6.98 us
    reshape x2, local copies, waits for them, and re-layouts, local(): jnp.repeat(jnp.repeat(cotangent.astype(jnp.float32), 2, axis=1), 2, axis=2)  6.82 us
    dot_general x9, matrix products, forward_conv(): jnp.dot(window, kernel[3 * row_off + col_off], preferred_element_type=jnp...  6.79 us
  transfers between devices with their start and end apart: 13, of which 4 were waited for; matrix products, arithmetic and copies ran while one was open for 21% of the time, Pallas kernels for 0%

commit v1 on v0

--- a/solution.py
+++ b/solution.py
@@ -126,7 +126,7 @@
     )
     kernel_part = kernel_grad(padded, grad_pre, rows, cols)
     bias_part = jnp.sum(grad_pre.astype(jnp.float32), axis=(0, 1, 2))
-    grad_kernel, grad_bias = lax.psum((kernel_part, bias_part), ("lat", "lon"))
+    grad_kernel, grad_bias = lax.psum(lax.psum((kernel_part, bias_part), "lon"), "lat")
     grad_padded = extend(grad_pre)
     is_north = lat_place == 0
     is_south = lat_place == lat_count - 1

time: 245 us -> 316 us (1.29); the launches traced: 244 us -> 310 us
  waiting for transfers between devices: 60.1 us -> 136 us
  blocking collectives: 72.1 us -> 52.4 us
  matrix products: 27.7 us -> 31.9 us
    psum x1 -> x2, waiting for transfers between devices: 57.3 us -> 133 us  [the longest x1 85.2 us: local(): lax.psum(lax.psum((kernel_part, bias_part), 'lon'), 'lat')]
    psum x1 -> x2, blocking collectives: 72.1 us -> 52.4 us  [the longest x1 32.3 us: local(): lax.psum((kernel_part, bias_part), 'lon')]
    dot_general x9, matrix products: 6.33 us -> 10.5 us  [back_conv(): lax.dot_general(window, kernel[3 * row_off + col_off], (((1,), (1,)), (()...]
    ppermute x4, starting transfers between devices: 5.03 us -> 8.8 us  [with_halo(): after = lax.ppermute(first, axis, down)]
    unnamed x45 -> x49, local copies, waits for them, and re-layouts: 8.65 us -> 9.37 us
  transfers between devices with their start and end apart: 13 -> 14, of which waited for: 4 -> 6; matrix products, arithmetic and copies ran while one was open for 21% -> 18% of each run, Pallas kernels for 0% -> 0%
where the time goes in v1:
time: 316 us; the launch traced here: 310 us
  waiting for transfers between devices  136 us (43%)
  blocking collectives  52.4 us (17%)
  matrix products  31.9 us (10%)
  local copies, waits for them, and re-layouts  31.6 us (10%)
  starting transfers between devices  26.3 us (8%)
  other arithmetic  17.1 us (5%)
  between operations  14.5 us (5%)
    psum x1, waiting for transfers between devices, local(): lax.psum(lax.psum((kernel_part, bias_part), 'lon'), 'lat')  85.2 us
    psum x1, waiting for transfers between devices, local(): lax.psum((kernel_part, bias_part), 'lon')  48.2 us
    psum x1, blocking collectives, local(): lax.psum((kernel_part, bias_part), 'lon')  32.3 us
    psum x1, blocking collectives, local(): lax.psum(lax.psum((kernel_part, bias_part), 'lon'), 'lat')  20.1 us
    dot_general x9, matrix products, kernel_grad(): lax.dot_general(window, flat_grad, (((0,), (0,)), ((), ())), preferred_el...  13.5 us
    dot_general x9, matrix products, back_conv(): lax.dot_general(window, kernel[3 * row_off + col_off], (((1,), (1,)), (()...  10.5 us
    ppermute x4, starting transfers between devices, with_halo(): before = lax.ppermute(last, axis, up)  10.4 us
    unnamed x49, local copies, waits for them, and re-layouts  9.37 us
  transfers between devices with their start and end apart: 14, of which 6 were waited for; matrix products, arithmetic and copies ran while one was open for 18% of the time, Pallas kernels for 0%

profile of v1, /device:TPU:1, one launch (start us, length us, event | category | flops | bytes accessed | tf_op | source)
XLA Modules:
  0.0 310.1 jit_solution(3263121316336023986)
XLA Ops:
  8.0 3.6 %collective-permute-start.2 = (bf16[2,1,48,256]{3,2,1,0:T(8,128)(2,1)S(1)}, bf16[2,1,48,256]{3,2,1,0:T(8,128)(2,1)S(1)}, u32[]{:S(2)}, u32[]{:S(2)}) collective-permute-start(bf16[2,1,48,256]{3,2,1,0:T(8,128)(2,1)S(1)} %get-tuple-element.41), channel_id=1, source_target_pairs={{0,8},{1,9},{2,10},{3,11},{4,12},{5,13},{6,14},{7,15},{8,0},{9,1},... | collective-permute-start | bytes 147464 | tf_op jit(solution)/shard_map/ppermute | solution.py:10
  11.7 3.5 %collective-permute-start.1 = (bf16[2,1,48,256]{3,2,1,0:T(8,128)(2,1)S(1)}, bf16[2,1,48,256]{3,2,1,0:T(8,128)(2,1)S(1)}, u32[]{:S(2)}, u32[]{:S(2)}) collective-permute-start(bf16[2,1,48,256]{3,2,1,0:T(8,128)(2,1)S(1)} %get-tuple-element.41), channel_id=1, source_target_pairs={{0,16},{16,32},{32,48},{48,64},{64,80},{80,96},{96,112},{1,17},{17... | collective-permute-start | bytes 147464 | tf_op jit(solution)/shard_map/ppermute | solution.py:20
  18.5 1.7 broadcast_in_dim.22
  20.3 3.4 %reshape.184 = f32[3072,256]{1,0:T(8,128)} reshape(f32[2,32,24,2,256]{4,3,2,1,0:T(2,128)S(1)} %broadcast_in_dim.22) | data formatting | bytes 6291456 | tf_op jit(solution)/shard_map/reshape | solution.py:123
  23.7 3.4 %reshape.178 = f32[2,32,48,256]{3,2,1,0:T(8,128)} reshape(f32[2,32,24,2,256]{4,3,2,1,0:T(2,128)S(1)} %broadcast_in_dim.22) | data formatting | bytes 6291456 | tf_op jit(solution)/shard_map/reshape | solution.py:123
  28.8 1.6 collective-permute-start.5
  34.9 3.1 %fusion.104 = (bf16[2,32,48,256]{3,2,1,0:T(8,128)(2,1)S(1)}, bf16[2,32,48,256]{3,2,1,0:T(8,128)(2,1)S(1)}, bf16[2,32,48,256]{3,2,1,0:T(8,128)(2,1)S(1)}, bf16[2,...) fusion(bf16[2,34,49,256]{3,2,1,0:T(8,128)(2,1)S(1)} %get-tuple-element., ...), kind=kLoop, calls=%fused_computation.171 | loop fusion | bytes 18874368 | tf_op jit(solution)/shard_map/slice | solution.py:50
  43.4 2.2 convert_reduce_fusion
  49.2 2.8 collective-permute-start.6
  52.3 5.4 %collective-permute-start.7 = (bf16[2,1,48,256]{3,2,1,0:T(8,128)(2,1)}, bf16[2,1,48,256]{3,2,1,0:T(8,128)(2,1)}, u32[]{:S(2)}, u32[]{:S(2)}) collective-permute-start(bf16[2,1,48,256]{3,2,1,0:T(8,128)(2,1)} %get-tuple-element.38), channel_id=1, source_target_pairs={{0,16},{16,32},{32,48},{48,64},{64,80},{80,96},{96,112},{1,17},{17... | collective-permute-start | bytes 147464 | tf_op jit(solution)/shard_map/ppermute | solution.py:20
  59.0 5.2 %reshape.176 = f32[2,16,2,24,2,256]{5,4,3,2,1,0:T(2,128)} reshape(f32[3072,256]{1,0:T(8,128)} %copy-done.4) | data formatting | bytes 6291456 | tf_op jit(solution)/shard_map/reshape | solution.py:56
  64.2 2.8 fusion.31
  69.8 1.4 fusion.18
  77.3 3.1 %multiply_reduce_fusion = f32[2,16,24,256]{3,2,1,0:T(8,128)S(1)} fusion(f32[16,2]{1,0:T(8,128)S(1)} %add_cosine_fusion, f32[256]{0:T(256)S(1)} %copy-done.20, f32[2,16,2,24,2,256]{5,4,3,2,1,0:T(2,128)} %reshape.176), kind=kLoop, calls=%fused_computation.23 | loop fusion | flops 6881280 | bytes 3933312 | tf_op jit(solution)/shard_map/reduce_sum | solution.py:119
  81.3 32.3 %psum.30 = f32[256]{0:T(256)S(1)} all-reduce(f32[256]{0:T(256)S(1)} %copy-done.23), channel_id=1, replica_groups=mesh['lat'=8,'lon'=16] {'lon'}, use_global_device_ids=true, to_apply=%region_4.5 | all-reduce | flops 256 | bytes 2048 | tf_op jit(solution)/shard_map/psum | solution.py:129
  113.6 20.1 %psum.31 = f32[256]{0:T(256)} all-reduce(f32[256]{0:T(256)S(1)} %psum.30), channel_id=1, replica_groups=mesh['lat'=8,'lon'=16] {'lat'}, use_global_device_ids=true, to_apply=%region_5.6 | all-reduce | flops 256 | bytes 2048 | tf_op jit(solution)/shard_map/psum | solution.py:129
  135.7 4.6 %collective-permute-start.11 = (bf16[2,34,1,256]{3,2,1,0:T(2,128)(2,1)S(1)}, bf16[2,34,1,256]{3,2,1,0:T(2,128)(2,1)S(1)}, u32[]{:S(2)}, u32[]{:S(2)}) collective-permute-start(bf16[2,34,1,256]{3,2,1,0:T(2,128)(2,1)S(1)} %get-tuple-element.31), channel_id=1, source_target_pairs={{1,0},{2,1},{3,2},{4,3},{5,4},{6,5},{7,6},{8,7},{9,8},{10,9},{11,1... | collective-permute-start | bytes 104456 | tf_op jit(solution)/shard_map/ppermute | solution.py:21
  146.1 4.5 %pad_maximum_fusion.3 = (bf16[2,32,48,256]{3,2,1,0:T(8,128)(2,1)}, bf16[2,32,48,256]{3,2,1,0:T(8,128)(2,1)}, bf16[2,32,48,256]{3,2,1,0:T(8,128)(2,1)}, bf16[2,32...) fusion(bf16[2,32,50,256]{3,2,1,0:T(8,128)(2,1)S(1)} %slice-done, ...), kind=kLoop, calls=%fused_computation.51 | loop fusion | flops 18874368 | bytes 11177984 | tf_op jit(solution)/shard_map/concatenate | solution.py:136
  155.3 1.5 convolution_add_fusion.4
  156.8 2.2 convolution_add_fusion.3
  159.0 48.2 %all-reduce.3.cloned.1.call-done = f32[9,256,256]{2,1,0:T(8,128)} async-done(((f32[9,256,256]{2,1,0:T(8,128)}), f32[9,256,256]{2,1,0:T(8,128)}) %all-reduce.3.cloned.1.call-update) | async-done | bytes 2359312 | tf_op jit(solution)/shard_map/psum | solution.py:129
  207.2 3.1 convolution_add_fusion.2
  214.8 85.2 %all-reduce.5.cloned.1.call-done = f32[9,256,256]{2,1,0:T(8,128)} async-done(((f32[9,256,256]{2,1,0:T(8,128)}), f32[9,256,256]{2,1,0:T(8,128)}) %all-reduce.5.cloned.1.call-update) | async-done | bytes 2359312 | tf_op jit(solution)/shard_map/psum | solution.py:129
  300.0 3.2 %copy.46 = f32[9,256,256]{2,1,0:T(8,128)} copy(f32[9,256,256]{2,1,0:T(8,128)} %all-reduce.5.cloned.1.call-done) | data formatting | bytes 4718592
  (133 shorter events, 47.1 us)
Async XLA Ops:
  7.2 200.0 %all-reduce.3.cloned.1.call-start = ((), (), s32[]{:S(2)}) async-start(), calls=%async_computation | async-start | bytes 4718592 | tf_op jit(solution)/shard_map/psum | solution.py:129
  8.0 19.7 %collective-permute-start.2 = (bf16[2,1,48,256]{3,2,1,0:T(8,128)(2,1)S(1)}, bf16[2,1,48,256]{3,2,1,0:T(8,128)(2,1)S(1)}, u32[]{:S(2)}, u32[]{:S(2)}) collective-permute-start(bf16[2,1,48,256]{3,2,1,0:T(8,128)(2,1)S(1)} %get-tuple-element.41), channel_id=1, source_target_pairs={{0,8},{1,9},{2,10},{3,11},{4,12},{5,13},{6,14},{7,15},{8,0},{9,1},... | collective-permute-start | bytes 147464 | tf_op jit(solution)/shard_map/ppermute | solution.py:10
  11.7 16.1 %collective-permute-start.1 = (bf16[2,1,48,256]{3,2,1,0:T(8,128)(2,1)S(1)}, bf16[2,1,48,256]{3,2,1,0:T(8,128)(2,1)S(1)}, u32[]{:S(2)}, u32[]{:S(2)}) collective-permute-start(bf16[2,1,48,256]{3,2,1,0:T(8,128)(2,1)S(1)} %get-tuple-element.41), channel_id=1, source_target_pairs={{0,16},{16,32},{32,48},{48,64},{64,80},{80,96},{96,112},{1,17},{17... | collective-permute-start | bytes 147464 | tf_op jit(solution)/shard_map/ppermute | solution.py:20
  15.2 12.5 %collective-permute-start.3 = (bf16[2,1,48,256]{3,2,1,0:T(8,128)(2,1)S(1)}, bf16[2,1,48,256]{3,2,1,0:T(8,128)(2,1)S(1)}, u32[]{:S(2)}, u32[]{:S(2)}) collective-permute-start(bf16[2,1,48,256]{3,2,1,0:T(8,128)(2,1)S(1)} %get-tuple-element.42), channel_id=1, source_target_pairs={{16,0},{32,16},{48,32},{64,48},{80,64},{96,80},{112,96},{17,1},{33... | collective-permute-start | bytes 147464 | tf_op jit(solution)/shard_map/ppermute | solution.py:21
  16.5 11.3 %collective-permute-start = (bf16[2,1,48,256]{3,2,1,0:T(8,128)(2,1)S(1)}, bf16[2,1,48,256]{3,2,1,0:T(8,128)(2,1)S(1)}, u32[]{:S(2)}, u32[]{:S(2)}) collective-permute-start(bf16[2,1,48,256]{3,2,1,0:T(8,128)(2,1)S(1)} %get-tuple-element.42), channel_id=1, source_target_pairs={{0,8},{1,9},{2,10},{3,11},{4,12},{5,13},{6,14},{7,15},{8,0},{9,1},... | collective-permute-start | bytes 147464 | tf_op jit(solution)/shard_map/ppermute | solution.py:10
  17.3 9.9 %copy-start.17 = (f32[32]{0:T(128)}, f32[32]{0:T(128)S(1)}, u32[]{:S(2)}) copy-start(f32[32]{0:T(128)S(1)} %fusion.97) | copy-start | bytes 388
  27.8 5.9 %copy-start.14 = (bf16[2,1,48,256]{3,2,1,0:T(8,128)(2,1)}, bf16[2,1,48,256]{3,2,1,0:T(8,128)(2,1)S(1)}, u32[]{:S(2)}) copy-start(bf16[2,1,48,256]{3,2,1,0:T(8,128)(2,1)S(1)} %broadcast_select_fusion.1) | copy-start | bytes 147460
  28.5 5.2 %copy-start.16 = (bf16[2,1,48,256]{3,2,1,0:T(8,128)(2,1)}, bf16[2,1,48,256]{3,2,1,0:T(8,128)(2,1)S(1)}, u32[]{:S(2)}) copy-start(bf16[2,1,48,256]{3,2,1,0:T(8,128)(2,1)S(1)} %broadcast_select_fusion.3) | copy-start | bytes 147460
  28.6 3.3 %copy-start.8 = (bf16[9,256,256]{2,1,0:T(8,128)(2,1)S(1)}, bf16[9,256,256]{2,1,0:T(8,128)(2,1)}, u32[]{:S(2)}) copy-start(bf16[9,256,256]{2,1,0:T(8,128)(2,1)} %param.5) | copy-start | bytes 3538948
  28.8 4.8 %collective-permute-start.5 = (bf16[2,34,1,256]{3,2,1,0:T(2,128)(2,1)S(1)}, bf16[2,34,1,256]{3,2,1,0:T(2,128)(2,1)S(1)}, u32[]{:S(2)}, u32[]{:S(2)}) collective-permute-start(bf16[2,34,1,256]{3,2,1,0:T(2,128)(2,1)S(1)} %get-tuple-element.35), channel_id=1, source_target_pairs={{1,0},{2,1},{3,2},{4,3},{5,4},{6,5},{7,6},{8,7},{9,8},{10,9},{11,1... | collective-permute-start | bytes 104456 | tf_op jit(solution)/shard_map/ppermute | solution.py:21
  30.4 3.3 %collective-permute-start.4 = (bf16[2,34,1,256]{3,2,1,0:T(2,128)(2,1)S(1)}, bf16[2,34,1,256]{3,2,1,0:T(2,128)(2,1)S(1)}, u32[]{:S(2)}, u32[]{:S(2)}) collective-permute-start(bf16[2,34,1,256]{3,2,1,0:T(2,128)(2,1)S(1)} %get-tuple-element.36), channel_id=1, source_target_pairs={{0,1},{1,2},{2,3},{3,4},{4,5},{5,6},{6,7},{7,8},{8,9},{9,10},{10,1... | collective-permute-start | bytes 104456 | tf_op jit(solution)/shard_map/ppermute | solution.py:20
  34.9 3.1 %copy-start.2 = (bf16[2,34,49,256]{3,2,1,0:T(8,128)(2,1)}, bf16[2,34,49,256]{3,2,1,0:T(8,128)(2,1)S(1)}, u32[]{:S(2)}) copy-start(bf16[2,34,49,256]{3,2,1,0:T(8,128)(2,1)S(1)} %get-tuple-element.33) | copy-start | bytes 5117956
  48.0 86.8 %collective-permute-start.9 = (bf16[2,1,48,256]{3,2,1,0:T(8,128)(2,1)}, bf16[2,1,48,256]{3,2,1,0:T(8,128)(2,1)}, u32[]{:S(2)}, u32[]{:S(2)}) collective-permute-start(bf16[2,1,48,256]{3,2,1,0:T(8,128)(2,1)} %get-tuple-element.37), channel_id=1, source_target_pairs={{16,0},{32,16},{48,32},{64,48},{80,64},{96,80},{112,96},{17,1},{33... | collective-permute-start | bytes 147464 | tf_op jit(solution)/shard_map/ppermute | solution.py:21
  49.2 84.5 %collective-permute-start.6 = (bf16[2,1,48,256]{3,2,1,0:T(8,128)(2,1)}, bf16[2,1,48,256]{3,2,1,0:T(8,128)(2,1)}, u32[]{:S(2)}, u32[]{:S(2)}) collective-permute-start(bf16[2,1,48,256]{3,2,1,0:T(8,128)(2,1)} %get-tuple-element.37), channel_id=1, source_target_pairs={{0,8},{1,9},{2,10},{3,11},{4,12},{5,13},{6,14},{7,15},{8,0},{9,1},... | collective-permute-start | bytes 147464 | tf_op jit(solution)/shard_map/ppermute | solution.py:10
  52.1 82.7 %collective-permute-start.8 = (bf16[2,1,48,256]{3,2,1,0:T(8,128)(2,1)}, bf16[2,1,48,256]{3,2,1,0:T(8,128)(2,1)}, u32[]{:S(2)}, u32[]{:S(2)}) collective-permute-start(bf16[2,1,48,256]{3,2,1,0:T(8,128)(2,1)} %get-tuple-element.38), channel_id=1, source_target_pairs={{0,8},{1,9},{2,10},{3,11},{4,12},{5,13},{6,14},{7,15},{8,0},{9,1},... | collective-permute-start | bytes 147464 | tf_op jit(solution)/shard_map/ppermute | solution.py:10
  52.3 81.4 %collective-permute-start.7 = (bf16[2,1,48,256]{3,2,1,0:T(8,128)(2,1)}, bf16[2,1,48,256]{3,2,1,0:T(8,128)(2,1)}, u32[]{:S(2)}, u32[]{:S(2)}) collective-permute-start(bf16[2,1,48,256]{3,2,1,0:T(8,128)(2,1)} %get-tuple-element.38), channel_id=1, source_target_pairs={{0,16},{16,32},{32,48},{48,64},{64,80},{80,96},{96,112},{1,17},{17... | collective-permute-start | bytes 147464 | tf_op jit(solution)/shard_map/ppermute | solution.py:20
  76.6 3.8 %copy-start.22 = (f32[16]{0:T(128)S(1)}, f32[16]{0:T(128)}, u32[]{:S(2)}) copy-start(f32[16]{0:T(128)} %copy-done.21) | copy-start | bytes 196
  76.6 4.7 %copy-start.23 = (f32[256]{0:T(256)S(1)}, f32[256]{0:T(256)}, u32[]{:S(2)}) copy-start(f32[256]{0:T(256)} %get-tuple-element.43) | copy-start | bytes 3076
  76.6 57.9 %copy-start.9 = (bf16[9,256,256]{2,1,0:T(8,128)(2,1)S(1)}, bf16[9,256,256]{2,1,0:T(8,128)(2,1)}, u32[]{:S(2)}) copy-start(bf16[9,256,256]{2,1,0:T(8,128)(2,1)} %param.5) | copy-start | bytes 3538948
  76.7 223.3 %all-reduce.5.cloned.1.call-start = ((), (), s32[]{:S(2)}) async-start(), calls=%async_computation.1 | async-start | bytes 4718592 | tf_op jit(solution)/shard_map/psum | solution.py:129
  135.7 5.6 %collective-permute-start.11 = (bf16[2,34,1,256]{3,2,1,0:T(2,128)(2,1)S(1)}, bf16[2,34,1,256]{3,2,1,0:T(2,128)(2,1)S(1)}, u32[]{:S(2)}, u32[]{:S(2)}) collective-permute-start(bf16[2,34,1,256]{3,2,1,0:T(2,128)(2,1)S(1)} %get-tuple-element.31), channel_id=1, source_target_pairs={{1,0},{2,1},{3,2},{4,3},{5,4},{6,5},{7,6},{8,7},{9,8},{10,9},{11,1... | collective-permute-start | bytes 104456 | tf_op jit(solution)/shard_map/ppermute | solution.py:21
  140.3 1.7 collective-permute-start.10
  152.4 2.9 copy-start.13
  207.2 3.1 %copy-start.11 = (bf16[2,32,48,256]{3,2,1,0:T(8,128)(2,1)S(1)}, bf16[2,32,48,256]{3,2,1,0:T(8,128)(2,1)}, u32[]{:S(2)}) copy-start(bf16[2,32,48,256]{3,2,1,0:T(8,128)(2,1)} %get-tuple-element.14) | copy-start | bytes 4718596
  (15 other events, 25.2 us)
Sparse Core Ops, SparseCore 0:
  76.7 130.4 all-reduce.2
  209.7 90.2 all-reduce.4
